TPU v7x, 128 devices: a whole 4x4x4 slice. The times are simulated.
128 devices in a mesh: expert: 32 (over y, x, core), tensor: 4 (over z).
Axes of the slice: x: 4, y: 4, z: 4, core: 2. Of those that a mesh axis runs over, the one named last changes fastest.
Arguments:
- tokens: bfloat16 [4096, 7168], P('expert', 'tensor'), may hold values from -6 to 6
- out_grad: bfloat16 [4096, 7168], P('expert', 'tensor'), may hold values from -6 to 6
- gate_weight: bfloat16 [32, 7168, 2048], P('expert', None, 'tensor'), may hold values from -0.0625 to 0.0625
- up_weight: bfloat16 [32, 7168, 2048], P('expert', None, 'tensor'), may hold values from -0.0625 to 0.0625
- proj_hidden: bfloat16 [2048, 64], P('tensor'), may hold values from -0.125 to 0.125
- proj_grad: bfloat16 [7168, 64], P('tensor'), may hold values from -0.0625 to 0.0625
- expert_ids: int32 [4096, 8], P('expert'), may hold values from 0 to 31, all different within a row; in each aligned block of 128 rows (0 to 127, 128 to 255, ...) at most 48 rows name the same one
- weight_index: int32 [4096, 8], P('expert'), may hold values from 0 to 63
- weight_table: float32 [64], replicated, may hold values from 0.02 to 0.4
- sequence_ids: int32 [4096], P('expert'), may hold values from 0 to 3, never falling along the last dimension, each value on 1 to 2048 neighbouring positions
Outputs:
- features: float32 [32, 4, 4096], P('expert', None, 'tensor')
Inputs may be any that keep to these rules, and one draw needn't show every extreme that they name: `expert_ids`: within each aligned block of 128 tokens no expert is named by more than 48 tokens, a bound that some block reaches. `sequence_ids`: document ids never fall along the tokens; every document is present.
All inputs are finite; a program needn't handle non-finite values.
Results may differ from a plain program's by a relative error of at most 0.0029.
Values may be sent and summed in bfloat16 or wider, within the bound.
No kernel may reach another device: no remote copies, remote signals or barrier semaphores. Data moves between devices by JAX's collectives and lax.ppermute only.
A program may use at most 192 MiB of HBM per device.

v0:
```python
import jax
import jax.numpy as jnp
from jax import lax
from jax.sharding import PartitionSpec as P

SEQS = 4


def slot_layout(expert_ids, weight_index, weight_table, sequence_ids, experts, capacity):
    tok_rows = expert_ids.shape[0]
    flat_ids = expert_ids.reshape(-1)
    picks = (flat_ids[:, None] == jnp.arange(experts, dtype=jnp.int32)[None, :]).astype(jnp.int32)
    running = jnp.cumsum(picks, axis=0) - 1
    slot_pos = jnp.sum(running * picks, axis=1)
    slot_index = flat_ids * capacity + slot_pos
    owners = jnp.arange(flat_ids.shape[0], dtype=jnp.int32) // expert_ids.shape[1]
    slot_token = jnp.full((experts * capacity,), tok_rows, jnp.int32).at[slot_index].set(owners)
    level_hits = (
        weight_index.reshape(-1)[:, None]
        == jnp.arange(weight_table.shape[0], dtype=jnp.int32)[None, :]
    )
    combine = jnp.sum(jnp.where(level_hits, weight_table[None, :], 0.0), axis=1)
    slot_weight = jnp.zeros((experts * capacity,), jnp.float32).at[slot_index].set(combine)
    slot_seq = (
        jnp.full((experts * capacity,), -1, jnp.int32).at[slot_index].set(sequence_ids[owners])
    )
    seq_weights = jnp.where(
        slot_seq[:, None] == jnp.arange(SEQS, dtype=jnp.int32)[None, :], slot_weight[:, None], 0.0
    )
    return (slot_token, seq_weights.reshape(experts, capacity, SEQS))


def pick_rows(source, slot_token, experts, capacity):
    padded = jnp.concatenate([source, jnp.zeros((1, source.shape[1]), source.dtype)], axis=0)
    return jnp.take(padded, slot_token, axis=0).reshape(experts, capacity, source.shape[1])


def local(
    tokens,
    out_grad,
    gate_weight,
    up_weight,
    proj_hidden,
    proj_grad,
    expert_ids,
    weight_index,
    weight_table,
    sequence_ids,
):
    experts = lax.axis_size("expert")
    tok_rows = tokens.shape[0]
    topk = expert_ids.shape[1]
    capacity = min(tok_rows, 3 * tok_rows * topk // (2 * experts))
    received = experts * capacity
    slot_token, seq_weights = slot_layout(
        expert_ids, weight_index, weight_table, sequence_ids, experts, capacity
    )
    source_rows = lax.all_gather(tokens, "tensor", axis=1, tiled=True)
    feature_send = pick_rows(source_rows, slot_token, experts, capacity)
    grad_send = pick_rows(out_grad, slot_token, experts, capacity)
    got_features, got_grads = (
        lax.all_to_all(feature_send, "expert", split_axis=0, concat_axis=0, tiled=True),
        lax.all_to_all(grad_send, "expert", split_axis=0, concat_axis=0, tiled=True),
    )
    got_weights = lax.all_to_all(seq_weights, "expert", split_axis=0, concat_axis=0, tiled=True)
    grad_part = jnp.dot(
        got_grads.reshape(received, -1), proj_grad, preferred_element_type=jnp.float32
    )
    projected = lax.psum(grad_part, "tensor")
    feature_block = got_features.reshape(received, -1)
    w_gate = gate_weight[0]
    w_up = up_weight[0]
    gate_sum = jnp.dot(feature_block, w_gate, preferred_element_type=jnp.float32)
    up_sum = jnp.dot(feature_block, w_up, preferred_element_type=jnp.float32)
    hidden = (jax.nn.silu(gate_sum) * up_sum).astype(jnp.bfloat16)
    left_part = jnp.dot(hidden, proj_hidden, preferred_element_type=jnp.float32)
    weights_flat = got_weights.reshape(received, SEQS)
    outer = jnp.einsum(
        "ts,tr,tq->srq", weights_flat, left_part, projected, precision=lax.Precision.HIGHEST
    )
    summed = lax.psum_scatter(outer.reshape(SEQS, -1), "tensor", scatter_dimension=1, tiled=True)
    return summed[None]


def solution(mesh):
    placed = (
        P("expert", "tensor"),
        P("expert", "tensor"),
        P("expert", None, "tensor"),
        P("expert", None, "tensor"),
        P("tensor", None),
        P("tensor", None),
        P("expert", None),
        P("expert", None),
        P(),
        P("expert"),
    )
    return jax.shard_map(
        local, mesh=mesh, in_specs=placed, out_specs=P("expert", None, "tensor"), check_vma=False
    )
```

profile of v0, /device:TPU:1, one launch (start us, length us, event | category | flops | bytes accessed | tf_op | source)
XLA Modules:
  0.0 499.4 jit_solution(4198014787959578296)
XLA Ops:
  6.5 0.0 copy-start
  6.5 0.0 copy-start.1
  6.5 0.0 all-gather.2.cloned.1.call-start
  6.5 0.7 all-gather.2.cloned.1.call-update
  7.3 0.8 copy.31
  8.1 0.1 eq.60
  8.1 0.1 eq.56
  8.2 0.7 broadcast_multiply_fusion
  9.0 9.0 %reduce-window.6 = s32[32,8,128]{2,1,0:T(8,128)S(1)} reduce-window(s32[32,8,128]{2,1,0:T(8,128)S(1)} %fusion.20, s32[]{:T(128)} %constant.60.clone.1), window={size=1x1x128 pad=0_0x0_0x127_0}, to_apply=%region_0.0 | reduce-window | flops 4161536 | bytes 262148 | tf_op jit(solution)/shard_map/reduce-window
  18.0 0.1 slice.14
  18.1 0.1 copy.33
  18.2 0.1 copy.34
  18.3 0.1 add_add_fusion
  18.4 0.1 copy.30
  18.5 0.1 mul.28
  18.6 0.8 copy.35
  19.4 0.1 eq.68
  19.6 0.8 select_reduce_fusion
  20.3 4.3 scatter_custom_fusion.2
  24.7 0.1 broadcast_in_dim.83
  24.7 5.9 %gather_fusion.1 = s32[1024]{0:T(1024)S(1)} fusion(s32[128]{0:T(128)} %param.19, s32[1024]{0:T(1024)S(1)} %broadcast_clamp_fusion), kind=kCustom, calls=%fused_computation.1 | custom fusion | bytes 12288 | tf_op jit(solution)/shard_map/gather | solution.py:25
  30.6 4.3 scatter_custom_fusion.1
  34.9 0.1 eq.64
  35.0 0.7 reshape.203
  35.8 8.6 %all-to-all-start.1 = ((f32[32,1,192]{2,1,0:T(1,128)}), f32[32,1,192]{2,1,0:T(1,128)S(1)}, u32[]{:S(2)}, u32[]{:S(2)}) async-start(f32[32,1,192]{2,1,0:T(1,128)} %reshape.203), calls=%async_computation.1 | async-start | bytes 65536 | tf_op jit(solution)/shard_map/all_to_all | solution.py:65
  44.4 4.3 scatter_custom_fusion
  48.7 0.1 broadcast_in_dim.75
  48.8 0.0 copy-done.1
  48.9 6.7 %gather_fusion.2 = bf16[1536,1792]{1,0:T(8,128)(2,1)} fusion(bf16[129,1792]{1,0:T(8,128)(2,1)S(1)} %concatenate.7, s32[2048]{0:T(1024)S(1)} %pad_clamp_fusion), kind=kCustom, calls=%fused_computation.2 | custom fusion | bytes 11016192 | tf_op jit(solution)/shard_map/jit(_take)/gather | solution.py:35
  55.6 5.6 %broadcast_select_fusion.1 = bf16[32,48,1792]{2,1,0:T(8,128)(2,1)} fusion(bf16[32,48,1792]{2,1,0:T(8,128)(2,1)} %bitcast.53, pred[32,48]{1,0:T(8,128)(4,1)S(1)} %broadcast_in_dim.75), kind=kLoop, calls=%fused_computation.11 | loop fusion | flops 2752512 | bytes 11011584 | tf_op jit(solution)/shard_map/jit(_take)/select_n | solution.py:35
  61.2 0.0 all-to-all-done.1
  61.2 7.4 %all-to-all-start.2 = ((bf16[32,48,1792]{2,1,0:T(8,128)(2,1)}), bf16[32,48,1792]{2,1,0:T(8,128)(2,1)}, u32[]{:S(2)}, u32[]{:S(2)}) async-start(bf16[32,48,1792]{2,1,0:T(8,128)(2,1)} %broadcast_select_fusion.1), calls=%async_computation.2 | async-start | bytes 11010048 | tf_op jit(solution)/shard_map/all_to_all | solution.py:63
  68.6 0.0 all-gather.2.cloned.1.call-done
  68.6 1.7 concatenate.6
  70.3 16.4 %gather_fusion = bf16[1536,7168]{1,0:T(8,128)(2,1)} fusion(bf16[129,7168]{1,0:T(8,128)(2,1)S(1)} %concatenate.6, s32[2048]{0:T(1024)S(1)} %pad_clamp_fusion), kind=kCustom, calls=%fused_computation | custom fusion | bytes 44046336 | tf_op jit(solution)/shard_map/jit(_take)/gather | solution.py:35
  86.7 19.3 %broadcast_select_fusion = bf16[32,48,7168]{2,1,0:T(8,128)(2,1)} fusion(bf16[32,48,7168]{2,1,0:T(8,128)(2,1)} %bitcast.52, pred[32,48]{1,0:T(8,128)(4,1)S(1)} %broadcast_in_dim.75), kind=kLoop, calls=%fused_computation.6 | loop fusion | flops 11010048 | bytes 44041728 | tf_op jit(solution)/shard_map/jit(_take)/select_n | solution.py:35
  106.1 27.3 %all-to-all-done.2 = bf16[32,48,1792]{2,1,0:T(8,128)(2,1)} async-done(((bf16[32,48,1792]{2,1,0:T(8,128)(2,1)}), bf16[32,48,1792]{2,1,0:T(8,128)(2,1)}, u32[]{:S(2)}, u32[]{:S(2)}) %all-to-all-start.2) | async-done | bytes 5505056 | tf_op jit(solution)/shard_map/all_to_all | solution.py:63
  133.4 9.3 %all-to-all-start = ((bf16[32,48,7168]{2,1,0:T(8,128)(2,1)}), bf16[32,48,7168]{2,1,0:T(8,128)(2,1)}, u32[]{:S(2)}, u32[]{:S(2)}) async-start(bf16[32,48,7168]{2,1,0:T(8,128)(2,1)} %broadcast_select_fusion), calls=%async_computation | async-start | bytes 44040192 | tf_op jit(solution)/shard_map/all_to_all | solution.py:62
  142.7 0.0 all-reduce.4.cloned.1.call-start
  142.7 0.5 broadcast.168
  143.2 0.7 reduce
  144.0 0.1 reshape.204
  144.1 0.1 reshape.141
  144.2 0.0 copy-done
  144.2 5.1 %fusion.33 = f32[1536,64]{0,1:T(8,128)} fusion(bf16[1536,1792]{1,0:T(8,128)(2,1)} %bitcast.10, bf16[1792,64]{0,1:T(8,128)(2,1)S(1)} %copy-done), kind=kOutput, calls=%fused_computation.57 | convolution fusion | flops 352321536 | bytes 6127616 | tf_op jit(solution)/shard_map/dot_general | solution.py:66
  149.3 0.0 all-reduce.4.cloned.1.call-update
  149.3 0.2 reduce-scatter.4.cloned.1.call-start
  149.6 258.5 %all-to-all-done = bf16[32,48,7168]{2,1,0:T(8,128)(2,1)} async-done(((bf16[32,48,7168]{2,1,0:T(8,128)(2,1)}), bf16[32,48,7168]{2,1,0:T(8,128)(2,1)}, u32[]{:S(2)}, u32[]{:S(2)}) %all-to-all-start) | async-done | bytes 22020128 | tf_op jit(solution)/shard_map/all_to_all | solution.py:62
  408.1 17.1 %fusion.2 = f32[1536,512]{1,0:T(8,128)S(1)} fusion(bf16[1536,7168]{1,0:T(8,128)(2,1)} %bitcast.5, bf16[1,7168,512]{2,1,0:T(8,128)(2,1)} %param.12), kind=kOutput, calls=%fused_computation.9 | convolution fusion | flops 11274289152 | bytes 32505856 | tf_op jit(solution)/shard_map/dot_general | solution.py:73
  425.2 0.0 copy-start.2
  425.2 18.3 %fusion.7 = bf16[1536,512]{1,0:T(8,128)(2,1)S(1)} fusion(bf16[1536,7168]{1,0:T(8,128)(2,1)} %bitcast.5, bf16[1,7168,512]{2,1,0:T(8,128)(2,1)} %param.13, f32[1536,512]{1,0:T(8,128)S(1)} %fusion.2), kind=kOutput, calls=%fused_computation.13 | convolution fusion | flops 11279007744 | bytes 34078720 | tf_op jit(solution)/shard_map/dot_general | solution.py:74
  443.5 0.0 copy-done.2
  443.5 0.6 fusion.32
  444.1 0.0 all-reduce.4.cloned.1.call-done
  444.1 2.4 fusion.12
  446.5 2.1 copy.39
  448.6 0.0 reduce-scatter.4.cloned.1.call-update
  448.6 42.4 %reduce-scatter.4.cloned.1.call-done = f32[1024,4]{1,0:T(8,128)} async-done(((f32[4096,4]{1,0:T(8,128)}), f32[1024,4]{1,0:T(8,128)}) %reduce-scatter.4.cloned.1.call-update) | async-done | bytes 16400
  491.1 1.8 copy.38
  (14 shorter events, 0.2 us)
Async XLA Ops:
  6.5 137.7 %copy-start = (bf16[1792,64]{0,1:T(8,128)(2,1)S(1)}, bf16[1792,64]{0,1:T(8,128)(2,1)}, u32[]{:S(2)}) copy-start(bf16[1792,64]{0,1:T(8,128)(2,1)} %param.15) | copy-start | bytes 688132
  6.5 42.3 %copy-start.1 = (bf16[128,1792]{1,0:T(8,128)(2,1)S(1)}, bf16[128,1792]{1,0:T(8,128)(2,1)}, u32[]{:S(2)}) copy-start(bf16[128,1792]{1,0:T(8,128)(2,1)} %param.11) | copy-start | bytes 1376260
  6.5 62.1 %all-gather.2.cloned.1.call-start = ((), (), s32[]{:S(2)}) async-start(), calls=%async_computation.4 | async-start | bytes 2293760 | tf_op jit(solution)/shard_map/all_gather | solution.py:58
  35.8 25.4 %all-to-all-start.1 = ((f32[32,1,192]{2,1,0:T(1,128)}), f32[32,1,192]{2,1,0:T(1,128)S(1)}, u32[]{:S(2)}, u32[]{:S(2)}) async-start(f32[32,1,192]{2,1,0:T(1,128)} %reshape.203), calls=%async_computation.1 | async-start | bytes 65536 | tf_op jit(solution)/shard_map/all_to_all | solution.py:65
  61.2 72.2 %all-to-all-start.2 = ((bf16[32,48,1792]{2,1,0:T(8,128)(2,1)}), bf16[32,48,1792]{2,1,0:T(8,128)(2,1)}, u32[]{:S(2)}, u32[]{:S(2)}) async-start(bf16[32,48,1792]{2,1,0:T(8,128)(2,1)} %broadcast_select_fusion.1), calls=%async_computation.2 | async-start | bytes 11010048 | tf_op jit(solution)/shard_map/all_to_all | solution.py:63
  133.4 274.7 %all-to-all-start = ((bf16[32,48,7168]{2,1,0:T(8,128)(2,1)}), bf16[32,48,7168]{2,1,0:T(8,128)(2,1)}, u32[]{:S(2)}, u32[]{:S(2)}) async-start(bf16[32,48,7168]{2,1,0:T(8,128)(2,1)} %broadcast_select_fusion), calls=%async_computation | async-start | bytes 44040192 | tf_op jit(solution)/shard_map/all_to_all | solution.py:62
  142.7 301.5 %all-reduce.4.cloned.1.call-start = ((), (), s32[]{:S(2)}) async-start(), calls=%async_computation.5 | async-start | bytes 786432 | tf_op jit(solution)/shard_map/psum | solution.py:69
  149.3 341.7 %reduce-scatter.4.cloned.1.call-start = ((), (), s32[]{:S(2)}) async-start(), calls=%async_computation.6 | async-start | bytes 2621440
  425.2 18.3 %copy-start.2 = (bf16[512,64]{0,1:T(8,128)(2,1)S(1)}, bf16[512,64]{0,1:T(8,128)(2,1)}, u32[]{:S(2)}) copy-start(bf16[512,64]{0,1:T(8,128)(2,1)} %param.14) | copy-start | bytes 196612
Sparse Core Ops, SparseCore 0:
  9.0 31.8 all-gather.1
  149.4 43.4 all-reduce.3
  448.7 42.2 reduce-scatter.3
where the time goes:
time: 500 us; the launch traced here: 499 us
  waiting for transfers between devices  329 us (66%)
  local copies, waits for them, and re-layouts  51.6 us (10%)
  matrix products  43.5 us (9%)
  other arithmetic  36.4 us (7%)
  starting transfers between devices  25.6 us (5%)
  between operations  13.4 us (3%)
    all_to_all x1, waiting for transfers between devices, local(): lax.all_to_all(feature_send, 'expert', split_axis=0, concat_axis=0, tiled...  259 us
    unnamed x4, waiting for transfers between devices  43.2 us
    all_to_all x1, waiting for transfers between devices, local(): lax.all_to_all(grad_send, 'expert', split_axis=0, concat_axis=0, tiled=True)  27.3 us
    select_n x3, other arithmetic, pick_rows(): jnp.take(padded, slot_token, axis=0)  24.9 us
    gather x2, local copies, waits for them, and re-layouts, pick_rows(): jnp.take(padded, slot_token, axis=0)  23.1 us
    dot_general x1, matrix products, local(): up_sum = jnp.dot(feature_block, w_up, preferred_element_type=jnp.float32)  18.3 us
    dot_general x1, matrix products, local(): jnp.dot(feature_block, w_gate, preferred_element_type=jnp.float32)  17.1 us
  transfers between devices with their start and end apart: 6, of which 3 were waited for; matrix products, arithmetic and copies ran while one was open for 25% of the time, Pallas kernels for 0%

commit v1 on v0

v1 whole, which is shorter than its diff:
```python
import functools

import jax
import jax.numpy as jnp
from jax import lax
from jax.experimental import pallas as pl
from jax.experimental.pallas import tpu as pltpu
from jax.sharding import PartitionSpec as P


SEQS = 4
RING = 4
BOTH = ("expert", "tensor")

SOURCE = (0, -1, 1, 2)
TARGET = (0, 1, -1, 2)


def chip_pairs(dy, dx):
    return [
        (y * 8 + x * 2 + c, ((y + dy) % RING) * 8 + ((x + dx) % RING) * 2 + c)
        for y in range(RING)
        for x in range(RING)
        for c in range(2)
    ]


def z_pairs(step):
    return [(z, (z + step) % RING) for z in range(RING)]


def split_z_pairs(step):
    return [
        (e * RING + z, e * RING + (z + step * (1 - 2 * (e % 2))) % RING)
        for e in range(32)
        for z in range(RING)
    ]


def send(value, axis, step):
    if axis == "x":
        return lax.ppermute(value, "expert", chip_pairs(0, step))
    if axis == "y":
        return lax.ppermute(value, "expert", chip_pairs(step, 0))
    return lax.ppermute(value, "tensor", z_pairs(step))


def ring_pieces(value, axis):
    return [value] + [send(value, axis, step) for step in TARGET[1:]]


def expert_kernel(plan, place_ref, *refs):
    pieces, has_acc, last = plan
    refs = list(refs)
    take = lambda n: [refs.pop(0) for _ in range(n)]
    xs = take(len(pieces))
    gate, up = take(2)
    acc_in = take(2) if has_acc else None
    proj = take(1)[0] if last else None
    outs = take(1 if last else 2)
    x_bufs = take(len(pieces))
    w_bufs = take(len(pieces))
    acc_g, acc_u, sems = take(3)
    count = [0]

    def copy(src, dst):
        op = pltpu.make_async_copy(src, dst, sems.at[count[0]])
        count[0] += 1
        op.start()
        return op

    waits = []
    for p, segments in enumerate(pieces):
        ops = [copy(xs[p].at[:, pl.ds(0, x_bufs[p].shape[1])], x_bufs[p])]
        at = 0
        for z_at, row, width in segments:
            for n, w in enumerate((gate, up)):
                ops.append(
                    copy(
                        w.at[place_ref[z_at], pl.ds(row, width)],
                        w_bufs[p].at[n, pl.ds(at, width)],
                    )
                )
            at += width
        if p == 0 and has_acc:
            ops += [copy(acc_in[0], acc_g), copy(acc_in[1], acc_u)]
        waits.append(ops)

    rows = acc_g.shape[0]
    part = rows // 4
    for p in range(len(pieces)):
        for op in waits[p]:
            op.wait()

        @pl.loop(0, 4)
        def _(m):
            at = pl.ds(pl.multiple_of(m * part, part), part)
            x = x_bufs[p][at, :]
            for n, acc in enumerate((acc_g, acc_u)):
                got = jnp.dot(x, w_bufs[p][n], preferred_element_type=jnp.float32)
                if p == 0 and not has_acc:
                    acc[at, :] = got
                else:
                    acc[at, :] += got

    if last:

        @pl.loop(0, 4)
        def _(m):
            at = pl.ds(pl.multiple_of(m * part, part), part)
            g = acc_g[at, :]
            hidden = (g / (1.0 + jnp.exp(-g)) * acc_u[at, :]).astype(jnp.bfloat16)
            outs[0][at, :] = jnp.dot(hidden, proj[...], preferred_element_type=jnp.float32)
    else:
        ops = [copy(acc_g, outs[0]), copy(acc_u, outs[1])]
        for op in ops:
            op.wait()


def expert_step(place, pieces, gate, up, acc, proj):
    last = proj is not None
    width = gate.shape[-1]
    xs = [x for x, _ in pieces]
    plan = (tuple(tuple(segs) for _, segs in pieces), acc is not None, last)
    rows = xs[0].shape[0]
    depths = [sum(width for _, _, width in segs) for _, segs in pieces]
    hbm = pl.BlockSpec(memory_space=pltpu.HBM)
    vmem = pl.BlockSpec(memory_space=pltpu.VMEM)
    copies = sum(1 + 2 * len(segs) for _, segs in pieces) + 4
    bf = jnp.bfloat16
    return pl.pallas_call(
        functools.partial(expert_kernel, plan),
        in_specs=[pl.BlockSpec(memory_space=pltpu.SMEM)]
        + [hbm] * (len(xs) + 2 + (2 if acc is not None else 0))
        + ([vmem] if last else []),
        out_specs=vmem if last else [hbm, hbm],
        out_shape=jax.ShapeDtypeStruct((rows, proj.shape[-1]), jnp.float32)
        if last
        else [pltpu.HBM((rows, width), jnp.float32)] * 2,
        scratch_shapes=[pltpu.VMEM((rows, d), bf) for d in depths]
        + [pltpu.VMEM((2, d, width), bf) for d in depths]
        + [
            pltpu.VMEM((rows, width), jnp.float32),
            pltpu.VMEM((rows, width), jnp.float32),
            pltpu.SemaphoreType.DMA((copies,)),
        ],
        cost_estimate=pl.CostEstimate(
            flops=4 * width * rows * sum(depths),
            bytes_accessed=(2 * rows + 4 * width) * sum(depths) + 16 * rows * width,
            transcendentals=0,
        ),
    )(place, *xs, gate, up, *(acc or ()), *((proj,) if last else ()))


def relay(value):
    near = lax.ppermute(value, BOTH, split_z_pairs(1))
    other = lax.ppermute(value, BOTH, split_z_pairs(-1))
    far = lax.ppermute(near, BOTH, split_z_pairs(1))
    return near, other, far


def local(
    tokens,
    out_grad,
    gate_weight,
    up_weight,
    proj_hidden,
    proj_grad,
    expert_ids,
    weight_index,
    weight_table,
    sequence_ids,
):
    experts = lax.axis_size("expert")
    toks, shard = tokens.shape
    topk = expert_ids.shape[1]
    cap = min(toks, 3 * toks * topk // (2 * experts))
    slots = experts * cap
    feats = proj_hidden.shape[-1]
    c_d = shard * 2 // 7 // 128 * 128
    c_1 = (shard - c_d) // 2 // 128 * 128
    c_2 = shard - c_d - c_1
    e = lax.axis_index("expert")
    z = lax.axis_index("tensor")
    c = e % 2
    bf = jnp.bfloat16

    ids_t = expert_ids.T
    every = jnp.arange(experts, dtype=jnp.int32)
    hits = ids_t[None] == every[:, None, None]
    hit = jnp.any(hits, axis=1)
    index = jnp.arange(toks, dtype=jnp.int32)
    upto = (index[:, None] <= index[None, :]).astype(bf)
    count = jnp.dot(hit.astype(bf), upto, preferred_element_type=jnp.float32)
    slot = jnp.where(hit, count.astype(jnp.int32) - 1, -1)
    order = jnp.arange(cap, dtype=jnp.int32)
    chosen = slot[:, None, :] == order[None, :, None]
    picks = jnp.where(chosen, 1.0, 0.0).astype(bf).reshape(slots, toks)

    def pick(value):
        return jnp.dot(picks, value, preferred_element_type=jnp.float32).astype(bf)

    def exchange(value):
        value = lax.all_to_all(
            value.reshape(experts, cap, -1), "expert", 0, 0, tiled=True
        )
        return value.reshape(slots, -1)

    d_parts = ring_pieces(tokens[:, c_1 + c_2 :], "z")
    x1 = exchange(pick(tokens[:, :c_1]))
    x2 = pick(tokens[:, c_1 : c_1 + c_2])

    right_part = jnp.dot(out_grad, proj_grad, preferred_element_type=jnp.float32)
    rights = ring_pieces(right_part, "z")
    right = rights[0] + rights[1] + rights[2] + rights[3]
    levels = jnp.arange(weight_table.shape[0], dtype=jnp.int32)
    weights_t = jnp.sum(
        jnp.where(
            weight_index.T[:, :, None] == levels[None, None], weight_table[None, None], 0.0
        ),
        axis=2,
    )
    comb = jnp.sum(jnp.where(hits, weights_t[None], 0.0), axis=1)
    spread = jnp.where(chosen, comb[:, None, :], 0.0).reshape(slots, toks)
    routed = jnp.dot(spread, right, precision=lax.Precision.HIGHEST)
    documents = pick(jnp.broadcast_to(sequence_ids.astype(bf)[:, None], (toks, feats)))
    high = lax.reduce_precision(routed, 8, 7)
    rest = routed - high
    middle = lax.reduce_precision(rest, 8, 7)
    terms = jnp.concatenate([high, middle, rest - middle], axis=1).astype(bf)
    d_rows = pick(jnp.concatenate(d_parts, axis=1))
    d_sent = jnp.concatenate([d_rows, terms, documents], axis=1)
    x2, d_sent = lax.optimization_barrier((x2, d_sent))
    x2 = exchange(x2)
    d_got = exchange(d_sent)
    side = d_got[:, RING * c_d :].astype(jnp.float32)
    routed = side[:, :feats] + side[:, feats : 2 * feats] + side[:, 2 * feats : 3 * feats]
    slot_seq = side[:, 3 * feats : 3 * feats + 1]
    right_rows = jnp.concatenate(
        [jnp.where(slot_seq == s, routed, 0.0) for s in range(SEQS)], axis=1
    )

    near1, other1, far1 = relay(x1)
    near2, other2, far2 = relay(x2)
    way = 1 - 2 * c
    source = jnp.array(SOURCE, jnp.int32)
    place = jnp.concatenate(
        [(z + source) % RING, jnp.stack([z, z - way, z + way, z + 2]) % RING]
    ).astype(jnp.int32)
    w_gate = gate_weight.reshape(RING, shard, -1)
    w_up = up_weight.reshape(RING, shard, -1)
    one = lambda x, at: (x, [(at, 0, c_1)])
    two = lambda x, at: (x, [(at, c_1, c_2)])
    seg_d = [(r, c_1 + c_2, c_d) for r in range(RING)]
    acc = expert_step(place, [one(x1, 4), two(x2, 4)], w_gate, w_up, None, None)
    acc = expert_step(place, [one(near1, 5), one(other1, 6), one(far1, 7)], w_gate, w_up, acc, None)
    acc = expert_step(place, [two(near2, 5), two(other2, 6), two(far2, 7)], w_gate, w_up, acc, None)
    left = expert_step(place, [(d_got, seg_d)], w_gate, w_up, acc, proj_hidden)

    outer = lax.dot_general(
        left, right_rows, (((0,), (0,)), ((), ())), precision=lax.Precision.HIGHEST
    )
    share = feats // RING
    mine = lambda k: lax.dynamic_slice_in_dim(outer, ((z + k) % RING) * share, share, 0)
    summed = mine(0)
    for k in (1, 2, 3):
        summed = summed + lax.ppermute(mine(k), "tensor", z_pairs(k))
    return summed.reshape(share, SEQS, feats).transpose(1, 0, 2).reshape(1, SEQS, share * feats)


def solution(mesh):
    placed = (
        P("expert", "tensor"),
        P("expert", "tensor"),
        P("expert", None, "tensor"),
        P("expert", None, "tensor"),
        P("tensor", None),
        P("tensor", None),
        P("expert", None),
        P("expert", None),
        P(),
        P("expert"),
    )
    return jax.shard_map(
        local, mesh=mesh, in_specs=placed, out_specs=P("expert", None, "tensor"), check_vma=False
    )
```

time: 500 us -> 269 us (0.54)
  waiting for transfers between devices: 329 us -> 100 us
  Pallas kernels: 0 us -> 59.9 us
  blocking collectives: 0 us -> 36.4 us
  local copies, waits for them, and re-layouts: 51.6 us -> 17.7 us
  matrix products: 43.5 us -> 14.8 us
  other arithmetic: 36.4 us -> 8.26 us
  between operations: 13.4 us -> 0.29 us
    all_to_all x3 -> x2, waiting for transfers between devices: 286 us -> 0.01 us  [exchange(): lax.all_to_all(value.reshape(experts, cap, -1), 'expert', 0, 0, tiled=True)]
    ppermute x0 -> x15, waiting for transfers between devices: none -> 100 us  [the longest x2 79.1 us: relay(): near = lax.ppermute(value, BOTH, split_z_pairs(1))]
    pallas_call x0 -> x4, Pallas kernels: none -> 59.9 us  [expert_step(): pl.pallas_call(functools.partial(expert_kernel, plan), in_specs=[pl.Block...]
    unnamed x4 -> x0, waiting for transfers between devices: 43.2 us -> none
    all_to_all x0 -> x1, blocking collectives: none -> 36.4 us  [exchange(): lax.all_to_all(value.reshape(experts, cap, -1), 'expert', 0, 0, tiled=True)]
    gather x3 -> x0, local copies, waits for them, and re-layouts: 29 us -> none  [the longest x2 23.1 us: pick_rows(): jnp.take(padded, slot_token, axis=0)]
    dot_general x5 -> x8, matrix products: 43.5 us -> 14.8 us  [the longest x4 9.38 us: pick(): return jnp.dot(picks, value, preferred_element_type=jnp.float32).astype(bf)]
    select_n x6 -> x4, other arithmetic: 25 us -> 2.91 us  [the longest x2 1.66 us: local(): jnp.where(slot_seq == s, routed, 0.0)]
  transfers between devices with their start and end apart: 6 -> 17, of which waited for: 3 -> 8; matrix products, arithmetic and copies ran while one was open for 25% -> 10% of each run, Pallas kernels for 0% -> 16%
where the time goes in v1:
time: 269 us; the launch traced here: 266 us
  waiting for transfers between devices  100 us (37%)
  Pallas kernels  59.9 us (22%)
  blocking collectives  36.4 us (14%)
  starting transfers between devices  29 us (11%)
  local copies, waits for them, and re-layouts  17.7 us (7%)
  matrix products  14.8 us (6%)
  other arithmetic  8.26 us (3%)
    ppermute x2, waiting for transfers between devices, relay(): near = lax.ppermute(value, BOTH, split_z_pairs(1))  79.1 us
    pallas_call x4, Pallas kernels, expert_step(): pl.pallas_call(functools.partial(expert_kernel, plan), in_specs=[pl.Block...  59.9 us
    all_to_all x1, blocking collectives, exchange(): lax.all_to_all(value.reshape(experts, cap, -1), 'expert', 0, 0, tiled=True)  36.4 us
    ppermute x2, waiting for transfers between devices, relay(): far = lax.ppermute(near, BOTH, split_z_pairs(1))  18.4 us
    all_to_all x2, starting transfers between devices, exchange(): lax.all_to_all(value.reshape(experts, cap, -1), 'expert', 0, 0, tiled=True)  13.8 us
    concatenate x1, local copies, waits for them, and re-layouts, local(): d_sent = jnp.concatenate([d_rows, terms, documents], axis=1)  11.2 us
    dot_general x4, matrix products, pick(): return jnp.dot(picks, value, preferred_element_type=jnp.float32).astype(bf)  9.38 us
    ppermute x6, starting transfers between devices, send(): return lax.ppermute(value, 'tensor', z_pairs(step))  9.27 us
  transfers between devices with their start and end apart: 17, of which 8 were waited for; matrix products, arithmetic and copies ran while one was open for 10% of the time, Pallas kernels for 16%

profile of v1, /device:TPU:1, one launch (start us, length us, event | category | flops | bytes accessed | tf_op | source)
XLA Modules:
  0.0 266.4 jit_solution(5771261314210129069)
XLA Ops:
  0.0 0.8 fusion.22
  0.8 0.1 fusion.9
  0.9 0.8 select_reduce_fusion
  1.7 0.7 select_reduce_fusion.1
  2.5 0.1 eq.86
  2.6 1.2 bitcast_select_fusion
  3.7 2.9 %convolution_convert_fusion.1 = bf16[1536,640]{1,0:T(8,128)(2,1)} fusion(bf16[1536,128]{1,0:T(8,128)(2,1)S(1)} %get-tuple-element.37, bf16[128,1792]{1,0:T(8,128)(2,1)} %param.11), kind=kOutput, calls=%fused_computation.1 | convolution fusion | flops 252641280 | bytes 2523136 | tf_op jit(solution)/shard_map/dot_general | solution.py:201
  6.6 8.8 %all-to-all-start.2 = ((bf16[32,48,640]{2,1,0:T(8,128)(2,1)}), bf16[32,48,640]{2,1,0:T(8,128)(2,1)}, u32[]{:S(2)}, u32[]{:S(2)}) async-start(bf16[32,48,640]{2,1,0:T(8,128)(2,1)} %bitcast.14), calls=%async_computation.2 | async-start | bytes 3932160 | tf_op jit(solution)/shard_map/all_to_all | solution.py:204
  15.4 1.7 collective-permute-start
  17.1 2.2 collective-permute-start.1
  19.3 0.3 fusion.32
  19.6 0.0 copy-start.6
  19.6 0.1 collective-permute-start.3
  19.7 2.7 collective-permute-start.4
  22.3 0.0 collective-permute-start.5
  22.4 0.7 convolution_convert_fusion.2
  23.0 0.3 convolution_convert_fusion.3
  23.4 0.2 copy.30
  23.6 0.4 collective-permute-done.3
  24.0 2.6 collective-permute-start.2
  26.7 0.6 copy-done.8
  27.3 2.9 %fusion.19 = (bf16[1536,64]{0,1:T(8,128)(2,1)S(1)}, bf16[1536,64]{0,1:T(8,128)(2,1)}, bf16[1536,64]{0,1:T(8,128)(2,1)}) fusion(f32[1536,128]{1,0:T(8,128)} %get-tuple-element.36, f32[128,64]{0,1:T(8,128)} %copy-done.8, f32[128,64]{0,1:T(8,128)S(1)} %collective-permute-done.4, f32[128,64]{0,1:T(8,128)} %copy-done.6, f32[128,64]{0,1:T(8,128)S(1)} %collective-permute-done.3), kind=kOutput, calls=%fused_computation.37 | convolution fusion | flops 151707648 | bytes 1507328 | tf_op jit(solution)/shard_map/dot_general | solution.py:225
  30.2 1.1 copy.27
  31.3 1.9 copy.28
  33.2 0.9 copy.29
  34.1 0.0 collective-permute-done
  34.1 0.0 collective-permute-done.1
  34.1 0.0 collective-permute-done.2
  34.1 5.5 %convolution_convert_fusion = bf16[1536,2048]{1,0:T(8,128)(2,1)} fusion(bf16[1536,128]{1,0:T(8,128)(2,1)S(1)} %get-tuple-element.37, bf16[128,512]{1,0:T(8,128)(2,1)} %collective-permute-done.2, bf16[128,512]{1,0:T(8,128)(2,1)} %collective-permute-done.1, bf16[128,512]{1,0:T(8,128)(2,1)} %collective-permute-done, bf16[128,512]{1,0:T(8,128)(2,1)S(1)} %slice.25), kind=kOutput, calls=%fused_computation | convolution fusion | flops 810549248 | bytes 7208960 | tf_op jit(solution)/shard_map/dot_general | solution.py:201
  39.6 11.2 %concatenate.17 = bf16[1536,2304]{1,0:T(8,128)(2,1)} concatenate(bf16[1536,2048]{1,0:T(8,128)(2,1)} %convolution_convert_fusion, bf16[1536,64]{1,0:T(8,128)(2,1)S(1)} %copy.27, bf16[1536,64]{1,0:T(8,128)(2,1)} %copy.28, bf16[1536,64]{1,0:T(8,128)(2,1)} %copy.29, bf16[1536,64]{1,0:T(8,128)(2,1)S(1)} %copy.30), dimensions={1} | concatenate | bytes 14155776 | tf_op jit(solution)/shard_map/concatenate | solution.py:232
  50.9 36.4 %all_to_all.15 = bf16[32,48,640]{2,1,0:T(8,128)(2,1)} all-to-all(bf16[32,48,640]{2,1,0:T(8,128)(2,1)S(1)} %bitcast.43), channel_id=1, replica_groups=mesh['expert'=32,'tensor'=4] {'expert'}, dimensions={0} | all-to-all | bytes 3932160 | tf_op jit(solution)/shard_map/all_to_all | solution.py:204
  87.3 5.1 %all-to-all-start = ((bf16[32,48,2304]{2,1,0:T(8,128)(2,1)}), bf16[32,48,2304]{2,1,0:T(8,128)(2,1)}, u32[]{:S(2)}, u32[]{:S(2)}) async-start(bf16[32,48,2304]{2,1,0:T(8,128)(2,1)} %bitcast.42), calls=%async_computation | async-start | bytes 14155776 | tf_op jit(solution)/shard_map/all_to_all | solution.py:204
  92.4 0.2 collective-permute-start.9
  92.6 0.1 collective-permute-start.6
  92.7 1.3 collective-permute-start.10
  94.1 42.5 %collective-permute-done.9.refs_0_ = bf16[1536,640]{1,0:T(8,128)(2,1)} collective-permute-done((bf16[1536,640]{1,0:T(8,128)(2,1)}, bf16[1536,640]{1,0:T(8,128)(2,1)}, u32[]{:S(2)}, u32[]{:S(2)}) %collective-permute-start.9) | collective-permute-done | bytes 1966112 | tf_op jit(solution)/shard_map/ppermute | solution.py:156
  136.6 0.0 collective-permute-start.11
  136.6 1.5 collective-permute-start.7
  138.0 36.6 %collective-permute-done.6.refs_0_ = bf16[1536,640]{1,0:T(8,128)(2,1)} collective-permute-done((bf16[1536,640]{1,0:T(8,128)(2,1)S(1)}, bf16[1536,640]{1,0:T(8,128)(2,1)}, u32[]{:S(2)}, u32[]{:S(2)}) %collective-permute-start.6) | collective-permute-done | bytes 1966112 | tf_op jit(solution)/shard_map/ppermute | solution.py:156
  174.6 0.0 collective-permute-start.8
  174.7 0.8 copy.31.refs_5_
  175.4 0.1 and_select_fusion
  175.5 0.6 pad_add_fusion.place_ref
  176.1 11.2 %shard_map.109 = (f32[1536,512]{1,0:T(8,128)}, f32[1536,512]{1,0:T(8,128)}) custom-call(s32[8]{0:T(128)} %pad_add_fusion.place_ref, bf16[1536,640]{1,0:T(8,128)(2,1)} %bitcast.15.refs_0_, bf16[1536,640]{1,0:T(8,128)(2,1)} %bitcast.44, bf16[4,1792,512]{2,1,0:T(8,128)(2,1)} %bitcast.34, bf16[4,1792,512]{2,1,0:T(8,128)(2,1)} %bitcast.38), custom_call_target="tpu_custom_call" | custom-call | flops 4026531840 | bytes 19136512 | tf_op jit(solution)/shard_map/pallas_call | solution.py:131
  187.3 0.0 collective-permute-done.10.refs_1_
  187.3 13.5 %collective-permute-done.11.refs_2_ = bf16[1536,640]{1,0:T(8,128)(2,1)} collective-permute-done((bf16[1536,640]{1,0:T(8,128)(2,1)}, bf16[1536,640]{1,0:T(8,128)(2,1)}, u32[]{:S(2)}, u32[]{:S(2)}) %collective-permute-start.11) | collective-permute-done | bytes 1966112 | tf_op jit(solution)/shard_map/ppermute | solution.py:158
  200.8 16.2 %shard_map.110 = (f32[1536,512]{1,0:T(8,128)}, f32[1536,512]{1,0:T(8,128)}) custom-call(s32[8]{0:T(128)} %pad_add_fusion.place_ref, bf16[1536,640]{1,0:T(8,128)(2,1)} %collective-permute-done.9.refs_0_, bf16[1536,640]{1,0:T(8,128)(2,1)} %collective-permute-done.10.refs_1_, bf16[1536,640]{1,0:T(8,128)(2,1)} %collective-permute-done.11.refs_2_, ...), custom_call_target="tpu_custom_call" | custom-call | flops 6039797760 | bytes 22413312 | tf_op jit(solution)/shard_map/pallas_call | solution.py:131
  217.0 4.9 %collective-permute-done.8.refs_2_ = bf16[1536,640]{1,0:T(8,128)(2,1)} collective-permute-done((bf16[1536,640]{1,0:T(8,128)(2,1)}, bf16[1536,640]{1,0:T(8,128)(2,1)}, u32[]{:S(2)}, u32[]{:S(2)}) %collective-permute-start.8) | collective-permute-done | bytes 1966112 | tf_op jit(solution)/shard_map/ppermute | solution.py:158
  221.9 16.2 %shard_map.111 = (f32[1536,512]{1,0:T(8,128)}, f32[1536,512]{1,0:T(8,128)}) custom-call(s32[8]{0:T(128)} %pad_add_fusion.place_ref, bf16[1536,640]{1,0:T(8,128)(2,1)} %collective-permute-done.6.refs_0_, bf16[1536,640]{1,0:T(8,128)(2,1)} %collective-permute-done.7.refs_1_, bf16[1536,640]{1,0:T(8,128)(2,1)} %collective-permute-done.8.refs_2_, ...), custom_call_target="tpu_custom_call" | custom-call | flops 6039797760 | bytes 22413312 | tf_op jit(solution)/shard_map/pallas_call | solution.py:131
  238.2 1.2 slice_convert_fusion
  239.4 1.1 compare_reduce_fusion.3
  240.5 0.5 broadcast_select_fusion.3
  241.0 16.3 %shard_map.112 = f32[1536,64]{1,0:T(8,128)} custom-call(s32[8]{0:T(128)} %pad_add_fusion.place_ref, bf16[1536,2304]{1,0:T(8,128)(2,1)} %bitcast.9.refs_0_, bf16[4,1792,512]{2,1,0:T(8,128)(2,1)} %bitcast.37, bf16[4,1792,512]{2,1,0:T(8,128)(2,1)} %bitcast.41, f32[1536,512]{1,0:T(8,128)} %get-tuple-element.19.refs_3_, f32[1536,512]{1,0:T(8,128)} %get-tuple-element.20.refs_4_, ...), custom_call_target="tpu_custom_call" | custom-call | flops 6442450944 | bytes 23068672 | tf_op jit(solution)/shard_map/pallas_call | solution.py:131
  257.3 1.2 broadcast_select_fusion.2
  258.5 0.0 copy-start.1
  258.6 2.2 fusion
  260.7 0.1 collective-permute-start.12
  260.8 2.2 collective-permute-start.13
  263.0 0.5 collective-permute-start.14
  263.5 1.1 collective-permute-done.12
  264.6 0.5 collective-permute-done.13
  265.1 0.5 collective-permute-done.14
  265.6 0.1 reshape.52
  265.7 0.7 reshape.53
  (30 shorter events, 0.1 us)
Async XLA Ops:
  0.0 19.3 %copy-start = (bf16[128,1792]{1,0:T(8,128)(2,1)S(1)}, bf16[128,1792]{1,0:T(8,128)(2,1)}, u32[]{:S(2)}) copy-start(bf16[128,1792]{1,0:T(8,128)(2,1)} %param.12) | copy-start | bytes 1376260
  6.6 8.8 %copy-start.4 = (bf16[128,1792]{1,0:T(8,128)(2,1)S(1)}, bf16[128,1792]{1,0:T(8,128)(2,1)}, u32[]{:S(2)}) copy-start(bf16[128,1792]{1,0:T(8,128)(2,1)} %param.11) | copy-start | bytes 1376260
  6.6 12.7 %copy-start.5 = (bf16[1792,64]{0,1:T(8,128)(2,1)S(1)}, bf16[1792,64]{0,1:T(8,128)(2,1)}, u32[]{:S(2)}) copy-start(bf16[1792,64]{0,1:T(8,128)(2,1)} %param.16) | copy-start | bytes 688132
  6.6 15.8 %copy-start.10 = (s32[128]{0:T(128)S(1)}, s32[128]{0:T(128)}, u32[]{:S(2)}) copy-start(s32[128]{0:T(128)} %param.20) | copy-start | bytes 1540
  6.6 44.3 %all-to-all-start.2 = ((bf16[32,48,640]{2,1,0:T(8,128)(2,1)}), bf16[32,48,640]{2,1,0:T(8,128)(2,1)}, u32[]{:S(2)}, u32[]{:S(2)}) async-start(bf16[32,48,640]{2,1,0:T(8,128)(2,1)} %bitcast.14), calls=%async_computation.2 | async-start | bytes 3932160 | tf_op jit(solution)/shard_map/all_to_all | solution.py:204
  15.4 18.7 %collective-permute-start = (bf16[128,512]{1,0:T(8,128)(2,1)S(1)}, bf16[128,512]{1,0:T(8,128)(2,1)}, u32[]{:S(2)}, u32[]{:S(2)}) collective-permute-start(bf16[128,512]{1,0:T(8,128)(2,1)S(1)} %slice.25), channel_id=1, source_target_pairs={{0,1},{1,2},{2,3},{3,0},{4,5},{5,6},{6,7},{7,4},{8,9},{9,10},{10,1... | collective-permute-start | bytes 393224 | tf_op jit(solution)/shard_map/ppermute | solution.py:45
  17.1 17.0 %collective-permute-start.1 = (bf16[128,512]{1,0:T(8,128)(2,1)S(1)}, bf16[128,512]{1,0:T(8,128)(2,1)}, u32[]{:S(2)}, u32[]{:S(2)}) collective-permute-start(bf16[128,512]{1,0:T(8,128)(2,1)S(1)} %slice.25), channel_id=1, source_target_pairs={{0,3},{1,0},{2,1},{3,2},{4,7},{5,4},{6,5},{7,6},{8,11},{9,8},{10,9... | collective-permute-start | bytes 393224 | tf_op jit(solution)/shard_map/ppermute | solution.py:45
  19.6 7.1 %copy-start.6 = (f32[128,64]{0,1:T(8,128)}, f32[128,64]{0,1:T(8,128)S(1)}, u32[]{:S(2)}) copy-start(f32[128,64]{0,1:T(8,128)S(1)} %fusion.32) | copy-start | bytes 98308
  19.6 4.4 %collective-permute-start.3 = (f32[128,64]{0,1:T(8,128)S(1)}, f32[128,64]{0,1:T(8,128)S(1)}, u32[]{:S(2)}, u32[]{:S(2)}) collective-permute-start(f32[128,64]{0,1:T(8,128)S(1)} %fusion.32), channel_id=1, source_target_pairs={{0,1},{1,2},{2,3},{3,0},{4,5},{5,6},{6,7},{7,4},{8,9},{9,10},{10,1... | collective-permute-start | bytes 98312 | tf_op jit(solution)/shard_map/ppermute | solution.py:45
  19.7 7.0 %collective-permute-start.4 = (f32[128,64]{0,1:T(8,128)S(1)}, f32[128,64]{0,1:T(8,128)S(1)}, u32[]{:S(2)}, u32[]{:S(2)}) collective-permute-start(f32[128,64]{0,1:T(8,128)S(1)} %fusion.32), channel_id=1, source_target_pairs={{0,3},{1,0},{2,1},{3,2},{4,7},{5,4},{6,5},{7,6},{8,11},{9,8},{10,9... | collective-permute-start | bytes 98312 | tf_op jit(solution)/shard_map/ppermute | solution.py:45
  22.3 4.3 %collective-permute-start.5 = (f32[128,64]{0,1:T(8,128)S(1)}, f32[128,64]{0,1:T(8,128)S(1)}, u32[]{:S(2)}, u32[]{:S(2)}) collective-permute-start(f32[128,64]{0,1:T(8,128)S(1)} %fusion.32), channel_id=1, source_target_pairs={{0,2},{1,3},{2,0},{3,1},{4,6},{5,7},{6,4},{7,5},{8,10},{9,11},{10,... | collective-permute-start | bytes 98312 | tf_op jit(solution)/shard_map/ppermute | solution.py:45
  24.0 10.1 %collective-permute-start.2 = (bf16[128,512]{1,0:T(8,128)(2,1)S(1)}, bf16[128,512]{1,0:T(8,128)(2,1)}, u32[]{:S(2)}, u32[]{:S(2)}) collective-permute-start(bf16[128,512]{1,0:T(8,128)(2,1)S(1)} %slice.25), channel_id=1, source_target_pairs={{0,2},{1,3},{2,0},{3,1},{4,6},{5,7},{6,4},{7,5},{8,10},{9,11},{10,... | collective-permute-start | bytes 393224 | tf_op jit(solution)/shard_map/ppermute | solution.py:45
  26.7 0.6 copy-start.8
  87.3 5.3 %copy-start.2 = (bf16[32,48,640]{2,1,0:T(8,128)(2,1)S(1)}, bf16[32,48,640]{2,1,0:T(8,128)(2,1)}, u32[]{:S(2)}) copy-start(bf16[32,48,640]{2,1,0:T(8,128)(2,1)} %all_to_all.15) | copy-start | bytes 5898244
  87.3 87.3 %copy-start.7 = (bf16[512,64]{0,1:T(8,128)(2,1)S(1)}, bf16[512,64]{0,1:T(8,128)(2,1)}, u32[]{:S(2)}) copy-start(bf16[512,64]{0,1:T(8,128)(2,1)} %param.15) | copy-start | bytes 196612
  87.3 88.1 %copy-start.9 = (s32[4]{0:T(128)S(1)}, s32[4]{0:T(128)}, u32[]{:S(2)}) copy-start(s32[4]{0:T(128)} %constant.82.clone) | copy-start | bytes 52
  87.3 150.8 %all-to-all-start = ((bf16[32,48,2304]{2,1,0:T(8,128)(2,1)}), bf16[32,48,2304]{2,1,0:T(8,128)(2,1)}, u32[]{:S(2)}, u32[]{:S(2)}) async-start(bf16[32,48,2304]{2,1,0:T(8,128)(2,1)} %bitcast.42), calls=%async_computation | async-start | bytes 14155776 | tf_op jit(solution)/shard_map/all_to_all | solution.py:204
  92.4 44.2 %collective-permute-start.9 = (bf16[1536,640]{1,0:T(8,128)(2,1)}, bf16[1536,640]{1,0:T(8,128)(2,1)}, u32[]{:S(2)}, u32[]{:S(2)}) collective-permute-start(bf16[1536,640]{1,0:T(8,128)(2,1)} %bitcast.15.refs_0_), channel_id=1, source_target_pairs={{0,1},{1,2},{2,3},{3,0},{4,7},{5,4},{6,5},{7,6},{8,9},{9,10},{10,1... | collective-permute-start | bytes 5898248 | tf_op jit(solution)/shard_map/ppermute | solution.py:156
  92.6 82.0 %collective-permute-start.6 = (bf16[1536,640]{1,0:T(8,128)(2,1)S(1)}, bf16[1536,640]{1,0:T(8,128)(2,1)}, u32[]{:S(2)}, u32[]{:S(2)}) collective-permute-start(bf16[1536,640]{1,0:T(8,128)(2,1)S(1)} %bitcast.45), channel_id=1, source_target_pairs={{0,1},{1,2},{2,3},{3,0},{4,7},{5,4},{6,5},{7,6},{8,9},{9,10},{10,1... | collective-permute-start | bytes 5898248 | tf_op jit(solution)/shard_map/ppermute | solution.py:156
  92.7 94.6 %collective-permute-start.10 = (bf16[1536,640]{1,0:T(8,128)(2,1)}, bf16[1536,640]{1,0:T(8,128)(2,1)}, u32[]{:S(2)}, u32[]{:S(2)}) collective-permute-start(bf16[1536,640]{1,0:T(8,128)(2,1)} %bitcast.15.refs_0_), channel_id=1, source_target_pairs={{0,3},{1,0},{2,1},{3,2},{4,5},{5,6},{6,7},{7,4},{8,11},{9,8},{10,9... | collective-permute-start | bytes 5898248 | tf_op jit(solution)/shard_map/ppermute | solution.py:157
  136.6 64.3 %collective-permute-start.11 = (bf16[1536,640]{1,0:T(8,128)(2,1)}, bf16[1536,640]{1,0:T(8,128)(2,1)}, u32[]{:S(2)}, u32[]{:S(2)}) collective-permute-start(bf16[1536,640]{1,0:T(8,128)(2,1)} %collective-permute-done.9.refs_0_), channel_id=1, source_target_pairs={{0,1},{1,2},{2,3},{3,0},{4,7},{5,4},{6,5},{7,6},{8,9},{9,10},{10,1... | collective-permute-start | bytes 5898248 | tf_op jit(solution)/shard_map/ppermute | solution.py:158
  136.6 80.4 %collective-permute-start.7 = (bf16[1536,640]{1,0:T(8,128)(2,1)S(1)}, bf16[1536,640]{1,0:T(8,128)(2,1)}, u32[]{:S(2)}, u32[]{:S(2)}) collective-permute-start(bf16[1536,640]{1,0:T(8,128)(2,1)S(1)} %bitcast.46), channel_id=1, source_target_pairs={{0,3},{1,0},{2,1},{3,2},{4,5},{5,6},{6,7},{7,4},{8,11},{9,8},{10,9... | collective-permute-start | bytes 5898248 | tf_op jit(solution)/shard_map/ppermute | solution.py:157
  174.6 47.3 %collective-permute-start.8 = (bf16[1536,640]{1,0:T(8,128)(2,1)}, bf16[1536,640]{1,0:T(8,128)(2,1)}, u32[]{:S(2)}, u32[]{:S(2)}) collective-permute-start(bf16[1536,640]{1,0:T(8,128)(2,1)} %collective-permute-done.6.refs_0_), channel_id=1, source_target_pairs={{0,1},{1,2},{2,3},{3,0},{4,7},{5,4},{6,5},{7,6},{8,9},{9,10},{10,1... | collective-permute-start | bytes 5898248 | tf_op jit(solution)/shard_map/ppermute | solution.py:158
  257.3 1.2 copy-start.3
  258.5 7.9 %copy-start.1 = (bf16[128,1792]{1,0:T(8,128)(2,1)S(1)}, bf16[128,1792]{1,0:T(8,128)(2,1)}, u32[]{:S(2)}) copy-start(bf16[128,1792]{1,0:T(8,128)(2,1)} %param.12) | copy-start | bytes 1376260
  260.7 3.9 %collective-permute-start.12 = (f32[16,256]{1,0:T(8,128)S(1)}, f32[16,256]{1,0:T(8,128)S(1)}, u32[]{:S(2)}, u32[]{:S(2)}) collective-permute-start(f32[16,256]{1,0:T(8,128)S(1)} %get-tuple-element.33), channel_id=1, source_target_pairs={{0,1},{1,2},{2,3},{3,0},{4,5},{5,6},{6,7},{7,4},{8,9},{9,10},{10,1... | collective-permute-start | bytes 49160 | tf_op jit(solution)/shard_map/ppermute | solution.py:267
  260.8 4.3 %collective-permute-start.13 = (f32[16,256]{1,0:T(8,128)S(1)}, f32[16,256]{1,0:T(8,128)S(1)}, u32[]{:S(2)}, u32[]{:S(2)}) collective-permute-start(f32[16,256]{1,0:T(8,128)S(1)} %get-tuple-element.35), channel_id=1, source_target_pairs={{0,2},{1,3},{2,0},{3,1},{4,6},{5,7},{6,4},{7,5},{8,10},{9,11},{10,... | collective-permute-start | bytes 49160 | tf_op jit(solution)/shard_map/ppermute | solution.py:267
  263.0 2.6 collective-permute-start.14
